TPU v7x, 32 devices: a whole 2x2x4 slice. The times are simulated.
32 devices in a mesh: grp: 2 (over x), bus: 16 (over z, y, core).
Axes of the slice: x: 2, y: 2, z: 4, core: 2. Of those that a mesh axis runs over, the one named last changes fastest.
Arguments:
- series: bfloat16 [32, 2048, 1024], P(('grp', 'bus')), parts along dimension 0, may hold values from -6 to 6
- hour_ids: int32 [32], P(('grp', 'bus')), parts along dimension 0, may hold values from 0 to 23
- hour_table: bfloat16 [24, 1024], replicated, may hold values from -3 to 3
- norm_gain: float32 [1024], replicated, may hold values from 0.1 to 1.9
- bus_order: int32 [4096], P('grp'), parts along dimension 0, may hold values from 0 to 2047, each once
- w_query: bfloat16 [1024, 512], replicated, may hold values from -0.1875 to 0.1875
- w_key: bfloat16 [1024, 512], replicated, may hold values from -0.1875 to 0.1875
- w_value: bfloat16 [1024, 512], replicated, may hold values from -0.1875 to 0.1875
- score_scale: float32 [8], replicated, may hold values from 0.5 to 10, as said below
- neighbors: int32 [32, 3], P('grp'), parts along dimension 0, may hold values from -1 to 15, as said below
- grad_out: bfloat16 [32, 2048, 512], P('grp', 'bus'), parts along dimension 0, may hold values from -6 to 6
Outputs:
- key_grad: bfloat16 [32, 2048, 512], P('grp', 'bus'), parts along dimension 0
- value_grad: bfloat16 [32, 2048, 512], P('grp', 'bus'), parts along dimension 0
There are 2 independent parts, one for each index of `grp`. A program takes and returns all parts, laid end to end along the dimension named above; an argument that names none is the same for every part. Nothing has to cross between parts.
Inputs may be any that keep to these rules, and one draw needn't show every extreme that they name: `neighbors`: row b lists the key blocks read by query block b: entry 0 is b - 1 or -1, entry 1 is b, entry 2 is b + 1 or -1; -1 marks a block not read, and stands in entry 0 of row 0 and entry 2 of row 15. `score_scale`: positive temperatures of the heads.
All inputs are finite; a program needn't handle non-finite values.
Results may differ from a plain program's by a relative error of at most 0.018.
The roundings to bfloat16 on the way count: a program that leaves them out, or rounds other values in their place, can miss the bound.
Values may be sent and summed in bfloat16 or wider, within the bound.
No kernel may reach another device: no remote copies, remote signals or barrier semaphores. Data moves between devices by JAX's collectives and lax.ppermute only.
A program may use at most 256 MiB of HBM per device.

v0:
```python
import math
import jax
import jax.numpy as jnp
from jax import lax
from jax.sharding import PartitionSpec as P

EPSILON = 1e-05
NEG_FILL = -1e30


def with_halo(shard, sides, width):
    for axis, dim in sides:
        devices, length = (lax.axis_size(axis), shard.shape[dim])
        up = [(i, (i + 1) % devices) for i in range(devices - 1)]
        down = [(j, i) for i, j in up]
        last = lax.slice_in_dim(shard, length - width, length, axis=dim)
        leading = lax.slice_in_dim(shard, 0, width, axis=dim)
        before = lax.ppermute(last, axis, up)
        after = lax.ppermute(leading, axis, down)
        shard = jnp.concatenate([before, shard, after], axis=dim)
    return shard


def from_behind(value, axis, steps):
    count = lax.axis_size(axis)
    leading, last = (max(0, -steps), min(count, count - steps))
    return lax.ppermute(value, axis, [(source, source + steps) for source in range(leading, last)])


def split_heads(array, head_count):
    return array.reshape(array.shape[0], array.shape[1], head_count, array.shape[2] // head_count)


def over_groups(step_fn, arrays, group_size):
    stacked = tuple(
        (
            item.reshape((item.shape[0] // group_size, group_size) + item.shape[1:])
            for item in arrays
        )
    )
    results = lax.map(lambda pieces: step_fn(*pieces), stacked)
    return tuple((item.reshape((-1,) + item.shape[2:]) for item in results))


def reader_terms(queries, key_tiles, value_tiles, grad_rows, colvalid, head_scale):
    scores = (
        jnp.einsum("sihd,sjhd->shij", queries, key_tiles, preferred_element_type=jnp.float32)
        * head_scale[None, :, None, None]
    )
    scores = jnp.where(colvalid[None, None, None, :], scores, NEG_FILL)
    row_max = jnp.max(scores, axis=-1)
    log_total = row_max + jnp.log(jnp.sum(jnp.exp(scores - row_max[..., None]), axis=-1))
    weights = jnp.exp(scores - log_total[..., None])
    weights_b = weights.astype(jnp.bfloat16)
    attended = jnp.einsum(
        "shij,sjhd->sihd", weights_b, value_tiles, preferred_element_type=jnp.float32
    ).astype(jnp.bfloat16)
    row_dot = jnp.einsum("sihd,sihd->shi", grad_rows, attended, preferred_element_type=jnp.float32)
    dweights = jnp.einsum(
        "sihd,sjhd->shij", grad_rows, value_tiles, preferred_element_type=jnp.float32
    )
    dscores = (weights * (dweights - row_dot[..., None]) * head_scale[None, :, None, None]).astype(
        jnp.bfloat16
    )
    value_part = jnp.einsum(
        "shij,sihd->sjhd", weights_b, grad_rows, preferred_element_type=jnp.float32
    )
    key_part = jnp.einsum("shij,sihd->sjhd", dscores, queries, preferred_element_type=jnp.float32)
    return (log_total, row_dot, key_part.astype(jnp.bfloat16), value_part.astype(jnp.bfloat16))


def on_device(
    series,
    hour_ids,
    hour_table,
    norm_gain,
    bus_order,
    w_query,
    w_key,
    w_value,
    score_scale,
    neighbors,
    grad_out,
):
    head_count = score_scale.shape[0]
    snap_count = grad_out.shape[0]
    block_rows = grad_out.shape[1]
    feat_width = grad_out.shape[2]
    head_dim = feat_width // head_count
    ordered = jnp.take(series, bus_order, axis=1)
    onehot = (
        hour_ids[:, None] == jnp.arange(hour_table.shape[0], dtype=jnp.int32)[None, :]
    ).astype(jnp.bfloat16)
    hour_rows = jnp.dot(onehot, hour_table, preferred_element_type=jnp.float32)
    mixed = ordered.astype(jnp.float32) + hour_rows[:, None, :]
    normed = (
        mixed * lax.rsqrt(jnp.mean(mixed * mixed, axis=-1, keepdims=True) + EPSILON) * norm_gain
    ).astype(jnp.bfloat16)
    arrived = lax.all_to_all(normed, "bus", split_axis=1, concat_axis=0, tiled=True)
    flat_rows = arrived.reshape(-1, arrived.shape[2])
    queries, key_rows, value_rows = [
        jnp.dot(flat_rows, weight, preferred_element_type=jnp.float32)
        .astype(jnp.bfloat16)
        .reshape(snap_count, block_rows, feat_width)
        for weight in (w_query, w_key, w_value)
    ]
    dev_index = lax.axis_index("bus")
    own_row = lax.dynamic_slice_in_dim(neighbors, dev_index, 1, 0)[0]
    colvalid = jnp.repeat(own_row >= 0, block_rows)
    head_scale = score_scale / math.sqrt(head_dim)
    group_size = math.gcd(snap_count, max(1, 512 // block_rows))
    kv_tiles = with_halo(jnp.stack([key_rows, value_rows]), (("bus", 2),), block_rows)
    query_heads = split_heads(queries, head_count)
    grad_heads = split_heads(grad_out, head_count)
    key_heads = split_heads(kv_tiles[0], head_count)
    value_heads = split_heads(kv_tiles[1], head_count)

    def full_step(query_part, key_part, value_part, grad_part):
        return reader_terms(query_part, key_part, value_part, grad_part, colvalid, head_scale)

    log_total, row_dot, key_part, value_part = over_groups(
        full_step, (query_heads, key_heads, value_heads, grad_heads), group_size
    )
    partials = jnp.stack(
        [
            key_part.reshape(snap_count, 3 * block_rows, feat_width),
            value_part.reshape(snap_count, 3 * block_rows, feat_width),
        ]
    )
    from_upper = from_behind(partials[:, :, :block_rows], "bus", -1)
    from_lower = from_behind(partials[:, :, 2 * block_rows :], "bus", 1)
    summed = (
        partials[:, :, block_rows : 2 * block_rows].astype(jnp.float32)
        + from_lower.astype(jnp.float32)
        + from_upper.astype(jnp.float32)
    )
    key_grad = summed[0].astype(jnp.bfloat16)
    value_grad = summed[1].astype(jnp.bfloat16)
    return (key_grad, value_grad)


def solution(mesh):
    return jax.shard_map(
        on_device,
        mesh=mesh,
        in_specs=(
            P(("grp", "bus"), None, None),
            P(("grp", "bus")),
            P(),
            P(),
            P("grp"),
            P(),
            P(),
            P(),
            P(),
            P("grp", None),
            P("grp", "bus", None),
        ),
        out_specs=(P("grp", "bus", None), P("grp", "bus", None)),
        check_vma=False,
    )
```

profile of v0, /device:TPU:12, one launch (start us, length us, event | category | flops | bytes accessed | tf_op | source)
XLA Modules:
  0.0 511.9 jit_solution(18104541909109588138)
XLA Ops:
  2.8 13.7 %gather_fusion = bf16[2048,1024]{1,0:T(8,128)(2,1)} fusion(bf16[2048,1024]{1,0:T(8,128)(2,1)} %bitcast.128, s32[2048]{0:T(1024)S(1)} %fusion.71), kind=kCustom, calls=%fused_computation | custom fusion | bytes 8396800 | tf_op jit(solution)/shard_map/jit(_take)/gather | solution.py:90
  16.6 3.6 multiply_reduce_fusion
  22.0 28.7 %copy.65 = bf16[1,2048,1024]{2,0,1:T(2,128)(2,1)} copy(bf16[1,2048,1024]{2,1,0:T(8,128)(2,1)S(1)} %multiply_convert_fusion.6) | data formatting | bytes 8388608 | tf_op jit(solution)/shard_map/convert_element_type | solution.py:98
  51.3 25.9 %reduce.5 = bf16[2048,1024]{1,0:T(8,128)(2,1)} reduce(bf16[2048,1,1024]{2,1,0:T(2,128)(2,1)} %bitcast.129, bf16[]{:T(256)} %broadcast.169), dimensions={1}, to_apply=%bitcast.102.reduce_sub_computation | reduce | bytes 8388610
  77.2 11.4 %reshape.223 = bf16[16,2,65536]{2,1,0:T(2,128)(2,1)} reshape(bf16[2048,1024]{1,0:T(8,128)(2,1)} %reduce.5) | data formatting | bytes 8388608
  88.6 98.4 %all_to_all.4 = bf16[16,2,65536]{2,1,0:T(2,128)(2,1)} all-to-all(bf16[16,2,65536]{2,1,0:T(2,128)(2,1)} %reshape.223), channel_id=1, replica_groups=mesh['grp'=2,'bus'=16] {'bus'}, dimensions={0} | all-to-all | bytes 8388608 | tf_op jit(solution)/shard_map/all_to_all | solution.py:99
  187.0 12.3 %reshape.224 = bf16[2048,1,1024]{2,1,0:T(2,128)(2,1)} reshape(bf16[16,2,65536]{2,1,0:T(2,128)(2,1)} %all_to_all.4) | data formatting | bytes 8388608
  199.3 7.1 %fusion.65 = bf16[2048,512]{1,0:T(8,128)(2,1)} fusion(bf16[1024,512]{1,0:T(8,128)(2,1)S(1)} %copy-done, bf16[1,2048,1024]{2,0,1:T(2,128)(2,1)} %bitcast.135), kind=kOutput, calls=%fused_computation.64 | convolution fusion | flops 2148532224 | bytes 7340032 | tf_op jit(solution)/shard_map/dot_general | solution.py:102
  209.5 7.3 %fusion.68 = bf16[2048,512]{1,0:T(8,128)(2,1)} fusion(bf16[1024,512]{1,0:T(8,128)(2,1)} %param.20, bf16[1,2048,1024]{2,0,1:T(2,128)(2,1)} %bitcast.136), kind=kOutput, calls=%fused_computation.65 | convolution fusion | flops 2148532224 | bytes 7340032 | tf_op jit(solution)/shard_map/dot_general | solution.py:102
  216.8 3.9 copy.37
  220.7 3.9 pad_maximum_fusion.2
  226.9 3.6 collective-permute-start.1
  230.5 3.9 copy.38
  234.6 7.3 %fusion.62 = bf16[2048,512]{1,0:T(8,128)(2,1)} fusion(bf16[1024,512]{1,0:T(8,128)(2,1)} %param.18, bf16[1,2048,1024]{2,0,1:T(2,128)(2,1)} %bitcast.137), kind=kOutput, calls=%fused_computation.63 | convolution fusion | flops 2148532224 | bytes 7340032 | tf_op jit(solution)/shard_map/dot_general | solution.py:102
  241.9 6.1 %reshape.221 = bf16[4,4,128,8,64]{4,3,2,1,0:T(8,128)(2,1)} reshape(bf16[2048,512]{1,0:T(8,128)(2,1)} %fusion.62) | data formatting | bytes 4194304 | tf_op jit(solution)/shard_map/reshape;reshape;reshape | solution.py:37
  248.1 5.1 copy.39
  253.1 66.6 %collective-permute-done = bf16[2,16,128,512]{2,3,1,0:T(8,128)(2,1)} collective-permute-done((bf16[2,16,128,512]{2,3,1,0:T(8,128)(2,1)}, bf16[2,16,128,512]{2,3,1,0:T(8,128)(2,1)}, u32[]{:S(2)}, u32[]{:S(2)}) %collective-permute-start) | collective-permute-done | bytes 4194336 | tf_op jit(solution)/shard_map/ppermute | solution.py:18
  319.7 6.3 %pad_maximum_fusion = bf16[2,16,384,512]{2,3,1,0:T(8,128)(2,1)S(1)} fusion(bf16[2,16,128,512]{2,3,1,0:T(8,128)(2,1)} %collective-permute-done.1, bf16[1,16,128,512]{2,3,1,0:T(8,128)(2,1)} %copy.37, bf16[1,16,128,512]{2,3,1,0:T(8,128)(2,1)S(1)} %copy.36, bf16[2,16,128,512]{2,3,1,0:T(8,128)(2,1)} %collective-permute-done), kind=kLoop, calls=%fused_computation.47 | loop fusion | flops 50331648 | bytes 25165824 | tf_op jit(solution)/shard_map/concatenate | solution.py:20
  326.1 5.9 %fusion.81 = (bf16[1,16,384,512]{2,3,1,0:T(8,128)(2,1)}, bf16[1,16,384,512]{2,3,1,0:T(8,128)(2,1)}) fusion(bf16[2,16,384,512]{2,3,1,0:T(8,128)(2,1)S(1)} %pad_maximum_fusion), kind=kLoop, calls=%fused_computation.83 | loop fusion | bytes 25165824 | tf_op jit(solution)/shard_map/slice | solution.py:116
  332.0 70.7 %while.13 = (s32[]{:T(128)}, bf16[4,4,384,8,64]{2,4,3,1,0:T(8,128)(2,1)}, bf16[4,4,384,8,64]{2,4,3,1,0:T(8,128)(2,1)}, bf16[4,4,128,8,64]{2,4,3,1,0:T(8,128)(2,1...) while((s32[]{:T(128)}, ...), condition=%wide.region_4.5_spmd.clone, body=%wide.region_1.0_spmd.clone.sunk | while | flops 1044111360 | bytes 75687264 | solution.py:41
  340.1 3.4 fusion.103
  343.5 6.2 %bitcast_dynamic-update-slice_fusion.4 = bf16[4,4,384,8,64]{2,4,3,1,0:T(8,128)(2,1)} fusion(bf16[4,4,384,8,64]{2,4,3,1,0:T(8,128)(2,1)} %get-tuple-element.211, s32[]{:T(128)} %get-tuple-element.210, f32[4,8,128,384]{3,2,1,0:T(8,128)} %copy-done.2, f32[4,8,128]{2,1,0:T(8,128)S(1)} %fusion.103, f32[4,8,128]{2,1,0:T(8,128)S(1)} %log_add_fusion.2, ...), kind=kOutput, calls=%fused_computation.14.clone.1 | convolution fusion | flops 414449664 | bytes 10521600 | tf_op jit(solution)/shard_map/while/body/eval_jaxpr/shij,sihd->sjhd/dot_general | solution.py:68
  357.7 3.4 fusion.103
  361.2 6.2 %bitcast_dynamic-update-slice_fusion.4 = bf16[4,4,384,8,64]{2,4,3,1,0:T(8,128)(2,1)} fusion(bf16[4,4,384,8,64]{2,4,3,1,0:T(8,128)(2,1)} %get-tuple-element.211, s32[]{:T(128)} %get-tuple-element.210, f32[4,8,128,384]{3,2,1,0:T(8,128)} %copy-done.2, f32[4,8,128]{2,1,0:T(8,128)S(1)} %fusion.103, f32[4,8,128]{2,1,0:T(8,128)S(1)} %log_add_fusion.2, ...), kind=kOutput, calls=%fused_computation.14.clone.1 | convolution fusion | flops 414449664 | bytes 10521600 | tf_op jit(solution)/shard_map/while/body/eval_jaxpr/shij,sihd->sjhd/dot_general | solution.py:68
  375.5 3.4 fusion.103
  378.9 6.2 %bitcast_dynamic-update-slice_fusion.4 = bf16[4,4,384,8,64]{2,4,3,1,0:T(8,128)(2,1)} fusion(bf16[4,4,384,8,64]{2,4,3,1,0:T(8,128)(2,1)} %get-tuple-element.211, s32[]{:T(128)} %get-tuple-element.210, f32[4,8,128,384]{3,2,1,0:T(8,128)} %copy-done.2, f32[4,8,128]{2,1,0:T(8,128)S(1)} %fusion.103, f32[4,8,128]{2,1,0:T(8,128)S(1)} %log_add_fusion.2, ...), kind=kOutput, calls=%fused_computation.14.clone.1 | convolution fusion | flops 414449664 | bytes 10521600 | tf_op jit(solution)/shard_map/while/body/eval_jaxpr/shij,sihd->sjhd/dot_general | solution.py:68
  393.1 3.4 fusion.103
  396.6 6.2 %bitcast_dynamic-update-slice_fusion.4 = bf16[4,4,384,8,64]{2,4,3,1,0:T(8,128)(2,1)} fusion(bf16[4,4,384,8,64]{2,4,3,1,0:T(8,128)(2,1)} %get-tuple-element.211, s32[]{:T(128)} %get-tuple-element.210, f32[4,8,128,384]{3,2,1,0:T(8,128)} %copy-done.2, f32[4,8,128]{2,1,0:T(8,128)S(1)} %fusion.103, f32[4,8,128]{2,1,0:T(8,128)S(1)} %log_add_fusion.2, ...), kind=kOutput, calls=%fused_computation.14.clone.1 | convolution fusion | flops 414449664 | bytes 10521600 | tf_op jit(solution)/shard_map/while/body/eval_jaxpr/shij,sihd->sjhd/dot_general | solution.py:68
  402.7 4.0 fusion.54
  409.3 3.5 collective-permute-start.3
  412.8 88.9 %collective-permute-done.2 = bf16[2,16,128,512]{2,3,1,0:T(8,128)(2,1)S(1)} collective-permute-done((bf16[2,16,128,512]{2,3,1,0:T(8,128)(2,1)S(1)}, bf16[2,16,128,512]{2,3,1,0:T(8,128)(2,1)S(1)}, u32[]{:S(2)}, u32[]{:S(2)}) %collective-permute-start.2) | collective-permute-done | bytes 4194336 | tf_op jit(solution)/shard_map/ppermute | solution.py:27
  505.4 3.9 copy.40
  (74 shorter events, 50.2 us)
Async XLA Ops:
  0.6 198.7 %copy-start = (bf16[1024,512]{1,0:T(8,128)(2,1)S(1)}, bf16[1024,512]{1,0:T(8,128)(2,1)}, u32[]{:S(2)}) copy-start(bf16[1024,512]{1,0:T(8,128)(2,1)} %param.19) | copy-start | bytes 3145732
  2.8 13.7 %copy-start.8 = (bf16[24,1024]{1,0:T(8,128)(2,1)S(1)}, bf16[24,1024]{1,0:T(8,128)(2,1)}, u32[]{:S(2)}) copy-start(bf16[24,1024]{1,0:T(8,128)(2,1)} %param.15) | copy-start | bytes 147460
  2.8 17.5 %copy-start.9 = (f32[1024]{0:T(1024)S(1)}, f32[1024]{0:T(1024)}, u32[]{:S(2)}) copy-start(f32[1024]{0:T(1024)} %param.16) | copy-start | bytes 12292
  16.5 3.8 copy-start.3
  220.7 13.7 %copy-start.10 = (s32[16,3]{0,1:T(4,128)S(1)}, s32[16,3]{0,1:T(4,128)}, u32[]{:S(2)}) copy-start(s32[16,3]{0,1:T(4,128)} %param.22) | copy-start | bytes 580
  220.7 13.9 %copy-start.11 = (f32[8]{0:T(128)S(1)}, f32[8]{0:T(128)}, u32[]{:S(2)}) copy-start(f32[8]{0:T(128)} %param.21) | copy-start | bytes 100
  224.7 95.1 %collective-permute-start = (bf16[2,16,128,512]{2,3,1,0:T(8,128)(2,1)}, bf16[2,16,128,512]{2,3,1,0:T(8,128)(2,1)}, u32[]{:S(2)}, u32[]{:S(2)}) collective-permute-start(bf16[2,16,128,512]{2,3,1,0:T(8,128)(2,1)} %pad_maximum_fusion.2), channel_id=1, source_target_pairs={{0,1},{1,2},{2,3},{3,4},{4,5},{5,6},{6,7},{7,8},{8,9},{9,10},{10,1... | collective-permute-start | bytes 12582920 | tf_op jit(solution)/shard_map/ppermute | solution.py:18
  226.9 92.9 %collective-permute-start.1 = (bf16[2,16,128,512]{2,3,1,0:T(8,128)(2,1)}, bf16[2,16,128,512]{2,3,1,0:T(8,128)(2,1)}, u32[]{:S(2)}, u32[]{:S(2)}) collective-permute-start(bf16[2,16,128,512]{2,3,1,0:T(8,128)(2,1)} %pad_maximum_fusion.2), channel_id=1, source_target_pairs={{1,0},{2,1},{3,2},{4,3},{5,4},{6,5},{7,6},{8,7},{9,8},{10,9},{11,1... | collective-permute-start | bytes 12582920 | tf_op jit(solution)/shard_map/ppermute | solution.py:19
  326.1 6.0 %copy-start.6 = (bf16[4,4,128,8,64]{2,4,3,1,0:T(8,128)(2,1)S(1)}, bf16[4,4,128,8,64]{2,4,3,1,0:T(8,128)(2,1)}, u32[]{:S(2)}) copy-start(bf16[4,4,128,8,64]{2,4,3,1,0:T(8,128)(2,1)} %copy.39) | copy-start | bytes 6291460
  332.1 5.1 %copy-start.7 = (bf16[4,4,128,8,64]{2,4,3,1,0:T(8,128)(2,1)S(1)}, bf16[4,4,128,8,64]{2,4,3,1,0:T(8,128)(2,1)}, u32[]{:S(2)}) copy-start(bf16[4,4,128,8,64]{2,4,3,1,0:T(8,128)(2,1)} %get-tuple-element.226) | copy-start | bytes 6291460 | tf_op jit(solution)/shard_map/while
  334.9 5.2 %copy-start.2 = (f32[4,8,128,384]{3,2,1,0:T(8,128)}, f32[4,8,128,384]{3,2,1,0:T(8,128)S(1)}, u32[]{:S(2)}) copy-start(f32[4,8,128,384]{3,2,1,0:T(8,128)S(1)} %get-tuple-element.198) | copy-start | bytes 18874372 | tf_op jit(solution)/shard_map/while
  349.7 5.1 %copy-start.7 = (bf16[4,4,128,8,64]{2,4,3,1,0:T(8,128)(2,1)S(1)}, bf16[4,4,128,8,64]{2,4,3,1,0:T(8,128)(2,1)}, u32[]{:S(2)}) copy-start(bf16[4,4,128,8,64]{2,4,3,1,0:T(8,128)(2,1)} %get-tuple-element.226) | copy-start | bytes 6291460 | tf_op jit(solution)/shard_map/while
  352.5 5.2 %copy-start.2 = (f32[4,8,128,384]{3,2,1,0:T(8,128)}, f32[4,8,128,384]{3,2,1,0:T(8,128)S(1)}, u32[]{:S(2)}) copy-start(f32[4,8,128,384]{3,2,1,0:T(8,128)S(1)} %get-tuple-element.198) | copy-start | bytes 18874372 | tf_op jit(solution)/shard_map/while
  367.4 5.1 %copy-start.7 = (bf16[4,4,128,8,64]{2,4,3,1,0:T(8,128)(2,1)S(1)}, bf16[4,4,128,8,64]{2,4,3,1,0:T(8,128)(2,1)}, u32[]{:S(2)}) copy-start(bf16[4,4,128,8,64]{2,4,3,1,0:T(8,128)(2,1)} %get-tuple-element.226) | copy-start | bytes 6291460 | tf_op jit(solution)/shard_map/while
  370.2 5.2 %copy-start.2 = (f32[4,8,128,384]{3,2,1,0:T(8,128)}, f32[4,8,128,384]{3,2,1,0:T(8,128)S(1)}, u32[]{:S(2)}) copy-start(f32[4,8,128,384]{3,2,1,0:T(8,128)S(1)} %get-tuple-element.198) | copy-start | bytes 18874372 | tf_op jit(solution)/shard_map/while
  385.1 5.1 %copy-start.7 = (bf16[4,4,128,8,64]{2,4,3,1,0:T(8,128)(2,1)S(1)}, bf16[4,4,128,8,64]{2,4,3,1,0:T(8,128)(2,1)}, u32[]{:S(2)}) copy-start(bf16[4,4,128,8,64]{2,4,3,1,0:T(8,128)(2,1)} %get-tuple-element.226) | copy-start | bytes 6291460 | tf_op jit(solution)/shard_map/while
  387.9 5.2 %copy-start.2 = (f32[4,8,128,384]{3,2,1,0:T(8,128)}, f32[4,8,128,384]{3,2,1,0:T(8,128)S(1)}, u32[]{:S(2)}) copy-start(f32[4,8,128,384]{3,2,1,0:T(8,128)S(1)} %get-tuple-element.198) | copy-start | bytes 18874372 | tf_op jit(solution)/shard_map/while
  402.7 99.0 %copy-start.4 = (bf16[4,4,384,8,64]{2,4,3,1,0:T(8,128)(2,1)S(1)}, bf16[4,4,384,8,64]{2,4,3,1,0:T(8,128)(2,1)}, u32[]{:S(2)}) copy-start(bf16[4,4,384,8,64]{2,4,3,1,0:T(8,128)(2,1)} %get-tuple-element.50) | copy-start | bytes 18874372
  402.7 99.0 %copy-start.5 = (bf16[4,4,384,8,64]{2,4,3,1,0:T(8,128)(2,1)S(1)}, bf16[4,4,384,8,64]{2,4,3,1,0:T(8,128)(2,1)}, u32[]{:S(2)}) copy-start(bf16[4,4,384,8,64]{2,4,3,1,0:T(8,128)(2,1)} %get-tuple-element.51) | copy-start | bytes 18874372
  406.7 95.0 %collective-permute-start.2 = (bf16[2,16,128,512]{2,3,1,0:T(8,128)(2,1)S(1)}, bf16[2,16,128,512]{2,3,1,0:T(8,128)(2,1)S(1)}, u32[]{:S(2)}, u32[]{:S(2)}) collective-permute-start(bf16[2,16,128,512]{2,3,1,0:T(8,128)(2,1)S(1)} %get-tuple-element.135), channel_id=1, source_target_pairs={{0,1},{1,2},{2,3},{3,4},{4,5},{5,6},{6,7},{7,8},{8,9},{9,10},{10,1... | collective-permute-start | bytes 12582920 | tf_op jit(solution)/shard_map/ppermute | solution.py:27
  409.3 92.4 %collective-permute-start.3 = (bf16[2,16,128,512]{2,3,1,0:T(8,128)(2,1)S(1)}, bf16[2,16,128,512]{2,3,1,0:T(8,128)(2,1)S(1)}, u32[]{:S(2)}, u32[]{:S(2)}) collective-permute-start(bf16[2,16,128,512]{2,3,1,0:T(8,128)(2,1)S(1)} %get-tuple-element.136), channel_id=1, source_target_pairs={{1,0},{2,1},{3,2},{4,3},{5,4},{6,5},{7,6},{8,7},{9,8},{10,9},{11,1... | collective-permute-start | bytes 12582920 | tf_op jit(solution)/shard_map/ppermute | solution.py:27
  503.7 8.2 %copy-start.1 = (bf16[1024,512]{1,0:T(8,128)(2,1)S(1)}, bf16[1024,512]{1,0:T(8,128)(2,1)}, u32[]{:S(2)}) copy-start(bf16[1024,512]{1,0:T(8,128)(2,1)} %param.19) | copy-start | bytes 3145732
where the time goes:
time: 513 us; the launch traced here: 512 us
  waiting for transfers between devices  156 us (30%)
  local copies, waits for them, and re-layouts  103 us (20%)
  blocking collectives  98.4 us (19%)
  matrix products  82.8 us (16%)
  other arithmetic  58.4 us (11%)
  starting transfers between devices  11.9 us (2%)
    all_to_all x1, blocking collectives, on_device(): lax.all_to_all(normed, 'bus', split_axis=1, concat_axis=0, tiled=True)  98.4 us
    ppermute x2, waiting for transfers between devices, from_behind(): lax.ppermute(value, axis, [(source, source + steps) for source in range(l...  88.9 us
    ppermute x1, waiting for transfers between devices, with_halo(): before = lax.ppermute(last, axis, up)  66.6 us
    unnamed x27, local copies, waits for them, and re-layouts  39.7 us
    convert_element_type x1, local copies, waits for them, and re-layouts, on_device(): normed = (mixed * lax.rsqrt(jnp.mean(mixed * mixed, axis=-1, keepdims=Tru...  28.7 us
    unnamed x1, other arithmetic  25.9 us
    dot_general x4, matrix products, reader_terms(): jnp.einsum('shij,sihd->sjhd', dscores, queries, preferred_element_type=jn...  24.6 us
    dot_general x3, matrix products, on_device(): jnp.dot(flat_rows, weight, preferred_element_type=jnp.float32)  21.8 us
  transfers between devices with their start and end apart: 4, of which 2 were waited for; matrix products, arithmetic and copies ran while one was open for 4% of the time, Pallas kernels for 0%

commit v1 on v0

--- a/solution.py
+++ b/solution.py
@@ -96,7 +96,27 @@
     normed = (
         mixed * lax.rsqrt(jnp.mean(mixed * mixed, axis=-1, keepdims=True) + EPSILON) * norm_gain
     ).astype(jnp.bfloat16)
-    arrived = lax.all_to_all(normed, "bus", split_axis=1, concat_axis=0, tiled=True)
+
+    def counts_see(tile_in, lane_axis):
+        y1, right_arr = (jax.lax.psum(1, axis_name=lane_axis), jax.lax.axis_index(lane_axis))
+        answer = tile_in.shape[1] // y1
+        tall = list(tile_in.shape)
+        tall[1] = answer
+        local_out = tall[0]
+        tall[0] = local_out * y1
+        t_next = jnp.zeros(tall, tile_in.dtype)
+        for t in range(y1):
+            r_now = lax.dynamic_slice_in_dim(tile_in, (right_arr ^ t) * answer, answer, axis=1)
+            if t:
+                r_now = jax.lax.ppermute(
+                    r_now, axis_name=lane_axis, perm=[(dev_i, dev_i ^ t) for dev_i in range(y1)]
+                )
+            t_next = lax.dynamic_update_slice_in_dim(
+                t_next, r_now, (right_arr ^ t) * local_out, axis=0
+            )
+        return t_next
+
+    arrived = counts_see(normed, "bus")
     flat_rows = arrived.reshape(-1, arrived.shape[2])
     queries, key_rows, value_rows = [
         jnp.dot(flat_rows, weight, preferred_element_type=jnp.float32)

time: 513 us -> 450 us (0.88)
  blocking collectives: 98.4 us -> 0 us
  waiting for transfers between devices: 156 us -> 238 us
  local copies, waits for them, and re-layouts: 103 us -> 73.2 us
  other arithmetic: 58.4 us -> 33.8 us
  starting transfers between devices: 11.9 us -> 23.5 us
    all_to_all x1 -> x0, blocking collectives: 98.4 us -> none  [on_device(): lax.all_to_all(normed, 'bus', split_axis=1, concat_axis=0, tiled=True)]
    ppermute x0 -> x15, waiting for transfers between devices: none -> 80.9 us  [counts_see(): jax.lax.ppermute(r_now, axis_name=lane_axis, perm=[(dev_i, dev_i ^ t) for...]
    convert_element_type x1 -> x0, local copies, waits for them, and re-layouts: 28.7 us -> none  [on_device(): normed = (mixed * lax.rsqrt(jnp.mean(mixed * mixed, axis=-1, keepdims=Tru...]
    unnamed x1 -> x2, other arithmetic: 25.9 us -> 0.01 us
    unnamed x27 -> x30, local copies, waits for them, and re-layouts: 39.7 us -> 17.6 us
    dynamic_update_slice x0 -> x15, local copies, waits for them, and re-layouts: none -> 15.6 us  [counts_see(): lax.dynamic_update_slice_in_dim(t_next, r_now, (right_arr ^ t) * local_ou...]
    ppermute x0 -> x15, starting transfers between devices: none -> 11.5 us  [counts_see(): jax.lax.ppermute(r_now, axis_name=lane_axis, perm=[(dev_i, dev_i ^ t) for...]
  transfers between devices with their start and end apart: 4 -> 19, of which waited for: 2 -> 13; matrix products, arithmetic and copies ran while one was open for 4% -> 8% of each run, Pallas kernels for 0% -> 0%
where the time goes in v1:
time: 450 us; the launch traced here: 448 us
  waiting for transfers between devices  238 us (53%)
  matrix products  78.2 us (17%)
  local copies, waits for them, and re-layouts  73.2 us (16%)
  other arithmetic  33.8 us (8%)
  starting transfers between devices  23.5 us (5%)
    ppermute x2, waiting for transfers between devices, from_behind(): lax.ppermute(value, axis, [(source, source + steps) for source in range(l...  89 us
    ppermute x15, waiting for transfers between devices, counts_see(): jax.lax.ppermute(r_now, axis_name=lane_axis, perm=[(dev_i, dev_i ^ t) for...  80.9 us
    ppermute x1, waiting for transfers between devices, with_halo(): before = lax.ppermute(last, axis, up)  67.7 us
    dot_general x4, matrix products, reader_terms(): jnp.einsum('shij,sihd->sjhd', dscores, queries, preferred_element_type=jn...  24.7 us
    dot_general x3, matrix products, on_device(): jnp.dot(flat_rows, weight, preferred_element_type=jnp.float32)  17.8 us
    unnamed x30, local copies, waits for them, and re-layouts  17.6 us
    dynamic_update_slice x15, local copies, waits for them, and re-layouts, counts_see(): lax.dynamic_update_slice_in_dim(t_next, r_now, (right_arr ^ t) * local_ou...  15.6 us
    dot_general x4, matrix products, reader_terms(): jnp.einsum('shij,sjhd->sihd', weights_b, value_tiles, preferred_element_t...  13.8 us
  transfers between devices with their start and end apart: 19, of which 13 were waited for; matrix products, arithmetic and copies ran while one was open for 8% of the time, Pallas kernels for 0%

profile of v1, /device:TPU:12, one launch (start us, length us, event | category | flops | bytes accessed | tf_op | source)
XLA Modules:
  0.0 448.2 jit_solution(12296448772029070610)
XLA Ops:
  2.9 13.7 %gather_fusion = bf16[2048,1024]{1,0:T(8,128)(2,1)} fusion(bf16[2048,1024]{1,0:T(8,128)(2,1)} %bitcast.116, s32[2048]{0:T(1024)S(1)} %fusion.56), kind=kCustom, calls=%fused_computation | custom fusion | bytes 8396800 | tf_op jit(solution)/shard_map/jit(_take)/gather | solution.py:90
  33.2 3.9 collective-permute-done.1
  52.3 7.2 %collective-permute-done.5 = bf16[1,128,1024]{2,1,0:T(8,128)(2,1)S(1)} collective-permute-done((bf16[1,128,1024]{2,1,0:T(8,128)(2,1)}, bf16[1,128,1024]{2,1,0:T(8,128)(2,1)S(1)}, u32[]{:S(2)}, u32[]{:S(2)}) %collective-permute-start.5) | collective-permute-done | bytes 262176 | tf_op jit(solution)/shard_map/ppermute | solution.py:111
  66.6 24.0 %collective-permute-done.8 = bf16[1,128,1024]{2,1,0:T(8,128)(2,1)S(1)} collective-permute-done((bf16[1,128,1024]{2,1,0:T(8,128)(2,1)S(1)}, bf16[1,128,1024]{2,1,0:T(8,128)(2,1)S(1)}, u32[]{:S(2)}, u32[]{:S(2)}) %collective-permute-start.8) | collective-permute-done | bytes 262176 | tf_op jit(solution)/shard_map/ppermute | solution.py:111
  91.2 10.5 %collective-permute-done.9 = bf16[1,128,1024]{2,1,0:T(8,128)(2,1)S(1)} collective-permute-done((bf16[1,128,1024]{2,1,0:T(8,128)(2,1)S(1)}, bf16[1,128,1024]{2,1,0:T(8,128)(2,1)S(1)}, u32[]{:S(2)}, u32[]{:S(2)}) %collective-permute-start.9) | collective-permute-done | bytes 262176 | tf_op jit(solution)/shard_map/ppermute | solution.py:111
  102.5 4.8 %collective-permute-done.10 = bf16[1,128,1024]{2,1,0:T(8,128)(2,1)S(1)} collective-permute-done((bf16[1,128,1024]{2,1,0:T(8,128)(2,1)S(1)}, bf16[1,128,1024]{2,1,0:T(8,128)(2,1)S(1)}, u32[]{:S(2)}, u32[]{:S(2)}) %collective-permute-start.10) | collective-permute-done | bytes 262176 | tf_op jit(solution)/shard_map/ppermute | solution.py:111
  108.0 10.6 %collective-permute-done.11 = bf16[1,128,1024]{2,1,0:T(8,128)(2,1)S(1)} collective-permute-done((bf16[1,128,1024]{2,1,0:T(8,128)(2,1)S(1)}, bf16[1,128,1024]{2,1,0:T(8,128)(2,1)S(1)}, u32[]{:S(2)}, u32[]{:S(2)}) %collective-permute-start.11) | collective-permute-done | bytes 262176 | tf_op jit(solution)/shard_map/ppermute | solution.py:111
  119.3 4.9 %collective-permute-done.12 = bf16[1,128,1024]{2,1,0:T(8,128)(2,1)S(1)} collective-permute-done((bf16[1,128,1024]{2,1,0:T(8,128)(2,1)S(1)}, bf16[1,128,1024]{2,1,0:T(8,128)(2,1)S(1)}, u32[]{:S(2)}, u32[]{:S(2)}) %collective-permute-start.12) | collective-permute-done | bytes 262176 | tf_op jit(solution)/shard_map/ppermute | solution.py:111
  124.9 4.9 %collective-permute-done.13 = bf16[1,128,1024]{2,1,0:T(8,128)(2,1)S(1)} collective-permute-done((bf16[1,128,1024]{2,1,0:T(8,128)(2,1)S(1)}, bf16[1,128,1024]{2,1,0:T(8,128)(2,1)S(1)}, u32[]{:S(2)}, u32[]{:S(2)}) %collective-permute-start.13) | collective-permute-done | bytes 262176 | tf_op jit(solution)/shard_map/ppermute | solution.py:111
  130.6 4.5 %collective-permute-done.14 = bf16[1,128,1024]{2,1,0:T(8,128)(2,1)S(1)} collective-permute-done((bf16[1,128,1024]{2,1,0:T(8,128)(2,1)S(1)}, bf16[1,128,1024]{2,1,0:T(8,128)(2,1)S(1)}, u32[]{:S(2)}, u32[]{:S(2)}) %collective-permute-start.14) | collective-permute-done | bytes 262176 | tf_op jit(solution)/shard_map/ppermute | solution.py:111
  135.8 5.8 %convolution_convert_fusion.2 = bf16[2048,512]{1,0:T(8,128)(2,1)} fusion(bf16[2048,1024]{1,0:T(8,128)(2,1)} %bitcast.127, bf16[1024,512]{1,0:T(8,128)(2,1)S(1)} %copy-done), kind=kOutput, calls=%fused_computation.58 | convolution fusion | flops 2148532224 | bytes 7340032 | tf_op jit(solution)/shard_map/dot_general | solution.py:122
  144.8 5.8 %convolution_convert_fusion.1 = bf16[2048,512]{1,0:T(8,128)(2,1)} fusion(bf16[2048,1024]{1,0:T(8,128)(2,1)} %bitcast.128, bf16[1024,512]{1,0:T(8,128)(2,1)S(1)} %copy-done.9), kind=kOutput, calls=%fused_computation.57 | convolution fusion | flops 2148532224 | bytes 7340032 | tf_op jit(solution)/shard_map/dot_general | solution.py:122
  150.6 3.9 copy.20
  154.5 3.9 pad_maximum_fusion.2
  160.5 3.8 collective-permute-start.16
  164.4 3.9 copy.21
  168.5 6.1 %convolution_convert_fusion.3 = bf16[2048,512]{1,0:T(8,128)(2,1)} fusion(bf16[2048,1024]{1,0:T(8,128)(2,1)} %bitcast.129, bf16[1024,512]{1,0:T(8,128)(2,1)} %param.18), kind=kOutput, calls=%fused_computation.59 | convolution fusion | flops 2148532224 | bytes 7340032 | tf_op jit(solution)/shard_map/dot_general | solution.py:122
  174.6 6.3 %reshape.217 = bf16[4,4,128,8,64]{4,3,2,1,0:T(8,128)(2,1)} reshape(bf16[2048,512]{1,0:T(8,128)(2,1)} %convolution_convert_fusion.3) | data formatting | bytes 4194304 | tf_op jit(solution)/shard_map/reshape;reshape;reshape | solution.py:37
  180.9 5.1 %copy.22 = bf16[4,4,128,8,64]{2,4,3,1,0:T(8,128)(2,1)} copy(bf16[4,4,128,8,64]{4,3,2,1,0:T(8,128)(2,1)} %reshape.217) | data formatting | bytes 4194304
  186.0 67.7 %collective-permute-done.15 = bf16[2,16,128,512]{2,3,1,0:T(8,128)(2,1)} collective-permute-done((bf16[2,16,128,512]{2,3,1,0:T(8,128)(2,1)}, bf16[2,16,128,512]{2,3,1,0:T(8,128)(2,1)}, u32[]{:S(2)}, u32[]{:S(2)}) %collective-permute-start.15) | collective-permute-done | bytes 4194336 | tf_op jit(solution)/shard_map/ppermute | solution.py:18
  253.7 6.3 %pad_maximum_fusion = bf16[2,16,384,512]{2,3,1,0:T(8,128)(2,1)S(1)} fusion(bf16[2,16,128,512]{2,3,1,0:T(8,128)(2,1)} %collective-permute-done.16, bf16[1,16,128,512]{2,3,1,0:T(8,128)(2,1)} %copy.20, bf16[1,16,128,512]{2,3,1,0:T(8,128)(2,1)S(1)} %copy.19, bf16[2,16,128,512]{2,3,1,0:T(8,128)(2,1)} %collective-permute-done.15), kind=kLoop, calls=%fused_computation.47 | loop fusion | flops 50331648 | bytes 25165824 | tf_op jit(solution)/shard_map/concatenate | solution.py:20
  260.0 5.8 %fusion.64 = (bf16[1,16,384,512]{2,3,1,0:T(8,128)(2,1)}, bf16[1,16,384,512]{2,3,1,0:T(8,128)(2,1)}) fusion(bf16[2,16,384,512]{2,3,1,0:T(8,128)(2,1)S(1)} %pad_maximum_fusion), kind=kLoop, calls=%fused_computation.106 | loop fusion | bytes 25165824 | tf_op jit(solution)/shard_map/slice | solution.py:136
  265.8 73.2 %while.13 = (s32[]{:T(128)}, bf16[4,4,384,8,64]{2,4,3,1,0:T(8,128)(2,1)}, bf16[4,4,384,8,64]{2,4,3,1,0:T(8,128)(2,1)}, bf16[4,4,128,8,64]{2,4,3,1,0:T(8,128)(2,1...) while((s32[]{:T(128)}, ...), condition=%wide.region_4.5_spmd.clone, body=%wide.region_1.0_spmd.clone.sunk | while | flops 1044111360 | bytes 75687264 | solution.py:41
  277.9 6.2 %bitcast_dynamic-update-slice_fusion.4 = bf16[4,4,384,8,64]{2,4,3,1,0:T(8,128)(2,1)} fusion(bf16[4,4,384,8,64]{2,4,3,1,0:T(8,128)(2,1)} %get-tuple-element.205, s32[]{:T(128)} %get-tuple-element.204, f32[4,8,128,384]{3,2,1,0:T(8,128)} %copy-done.2, f32[4,8,128]{2,1,0:T(8,128)S(1)} %fusion.89, f32[4,8,128]{2,1,0:T(8,128)S(1)} %log_add_fusion.2, ...), kind=kOutput, calls=%fused_computation.17.clone.1 | convolution fusion | flops 414449664 | bytes 10521600 | tf_op jit(solution)/shard_map/while/body/eval_jaxpr/shij,sihd->sjhd/dot_general | solution.py:68
  296.1 6.2 %bitcast_dynamic-update-slice_fusion.4 = bf16[4,4,384,8,64]{2,4,3,1,0:T(8,128)(2,1)} fusion(bf16[4,4,384,8,64]{2,4,3,1,0:T(8,128)(2,1)} %get-tuple-element.205, s32[]{:T(128)} %get-tuple-element.204, f32[4,8,128,384]{3,2,1,0:T(8,128)} %copy-done.2, f32[4,8,128]{2,1,0:T(8,128)S(1)} %fusion.89, f32[4,8,128]{2,1,0:T(8,128)S(1)} %log_add_fusion.2, ...), kind=kOutput, calls=%fused_computation.17.clone.1 | convolution fusion | flops 414449664 | bytes 10521600 | tf_op jit(solution)/shard_map/while/body/eval_jaxpr/shij,sihd->sjhd/dot_general | solution.py:68
  311.0 3.4 fusion.89
  314.4 6.2 %bitcast_dynamic-update-slice_fusion.4 = bf16[4,4,384,8,64]{2,4,3,1,0:T(8,128)(2,1)} fusion(bf16[4,4,384,8,64]{2,4,3,1,0:T(8,128)(2,1)} %get-tuple-element.205, s32[]{:T(128)} %get-tuple-element.204, f32[4,8,128,384]{3,2,1,0:T(8,128)} %copy-done.2, f32[4,8,128]{2,1,0:T(8,128)S(1)} %fusion.89, f32[4,8,128]{2,1,0:T(8,128)S(1)} %log_add_fusion.2, ...), kind=kOutput, calls=%fused_computation.17.clone.1 | convolution fusion | flops 414449664 | bytes 10521600 | tf_op jit(solution)/shard_map/while/body/eval_jaxpr/shij,sihd->sjhd/dot_general | solution.py:68
  332.8 6.2 %bitcast_dynamic-update-slice_fusion.4 = bf16[4,4,384,8,64]{2,4,3,1,0:T(8,128)(2,1)} fusion(bf16[4,4,384,8,64]{2,4,3,1,0:T(8,128)(2,1)} %get-tuple-element.205, s32[]{:T(128)} %get-tuple-element.204, f32[4,8,128,384]{3,2,1,0:T(8,128)} %copy-done.2, f32[4,8,128]{2,1,0:T(8,128)S(1)} %fusion.89, f32[4,8,128]{2,1,0:T(8,128)S(1)} %log_add_fusion.2, ...), kind=kOutput, calls=%fused_computation.17.clone.1 | convolution fusion | flops 414449664 | bytes 10521600 | tf_op jit(solution)/shard_map/while/body/eval_jaxpr/shij,sihd->sjhd/dot_general | solution.py:68
  338.9 4.0 fusion.54
  345.3 3.7 collective-permute-start.18
  349.0 89.0 %collective-permute-done.17 = bf16[2,16,128,512]{2,3,1,0:T(8,128)(2,1)S(1)} collective-permute-done((bf16[2,16,128,512]{2,3,1,0:T(8,128)(2,1)S(1)}, bf16[2,16,128,512]{2,3,1,0:T(8,128)(2,1)S(1)}, u32[]{:S(2)}, u32[]{:S(2)}) %collective-permute-start.17) | collective-permute-done | bytes 4194336 | tf_op jit(solution)/shard_map/ppermute | solution.py:27
  441.6 4.0 copy.24
  (123 shorter events, 104.0 us)
Async XLA Ops:
  0.6 135.2 %copy-start = (bf16[1024,512]{1,0:T(8,128)(2,1)S(1)}, bf16[1024,512]{1,0:T(8,128)(2,1)}, u32[]{:S(2)}) copy-start(bf16[1024,512]{1,0:T(8,128)(2,1)} %param.19) | copy-start | bytes 3145732
  2.9 13.7 %copy-start.6 = (bf16[24,1024]{1,0:T(8,128)(2,1)S(1)}, bf16[24,1024]{1,0:T(8,128)(2,1)}, u32[]{:S(2)}) copy-start(bf16[24,1024]{1,0:T(8,128)(2,1)} %param.15) | copy-start | bytes 147460
  27.7 3.5 collective-permute-start
  27.7 9.4 %collective-permute-start.1 = (bf16[1,128,1024]{2,1,0:T(8,128)(2,1)}, bf16[1,128,1024]{2,1,0:T(8,128)(2,1)}, u32[]{:S(2)}, u32[]{:S(2)}) collective-permute-start(bf16[1,128,1024]{2,1,0:T(8,128)(2,1)} %get-tuple-element.132), channel_id=1, source_target_pairs={{0,2},{1,3},{2,0},{3,1},{4,6},{5,7},{6,4},{7,5},{8,10},{9,11},{10,... | collective-permute-start | bytes 786440 | tf_op jit(solution)/shard_map/ppermute | solution.py:111
  28.2 13.8 %collective-permute-start.2 = (bf16[1,128,1024]{2,1,0:T(8,128)(2,1)}, bf16[1,128,1024]{2,1,0:T(8,128)(2,1)}, u32[]{:S(2)}, u32[]{:S(2)}) collective-permute-start(bf16[1,128,1024]{2,1,0:T(8,128)(2,1)} %get-tuple-element.131), channel_id=1, source_target_pairs={{0,3},{1,2},{2,1},{3,0},{4,7},{5,6},{6,5},{7,4},{8,11},{9,10},{10,... | collective-permute-start | bytes 786440 | tf_op jit(solution)/shard_map/ppermute | solution.py:111
  29.5 16.7 %collective-permute-start.3 = (bf16[1,128,1024]{2,1,0:T(8,128)(2,1)}, bf16[1,128,1024]{2,1,0:T(8,128)(2,1)}, u32[]{:S(2)}, u32[]{:S(2)}) collective-permute-start(bf16[1,128,1024]{2,1,0:T(8,128)(2,1)} %get-tuple-element.130), channel_id=1, source_target_pairs={{0,4},{1,5},{2,6},{3,7},{4,0},{5,1},{6,2},{7,3},{8,12},{9,13},{10,... | collective-permute-start | bytes 786440 | tf_op jit(solution)/shard_map/ppermute | solution.py:111
  30.0 18.1 %collective-permute-start.4 = (bf16[1,128,1024]{2,1,0:T(8,128)(2,1)}, bf16[1,128,1024]{2,1,0:T(8,128)(2,1)}, u32[]{:S(2)}, u32[]{:S(2)}) collective-permute-start(bf16[1,128,1024]{2,1,0:T(8,128)(2,1)} %get-tuple-element.129), channel_id=1, source_target_pairs={{0,5},{1,4},{2,7},{3,6},{4,1},{5,0},{6,3},{7,2},{8,13},{9,12},{10,... | collective-permute-start | bytes 786440 | tf_op jit(solution)/shard_map/ppermute | solution.py:111
  31.2 28.3 %collective-permute-start.5 = (bf16[1,128,1024]{2,1,0:T(8,128)(2,1)}, bf16[1,128,1024]{2,1,0:T(8,128)(2,1)S(1)}, u32[]{:S(2)}, u32[]{:S(2)}) collective-permute-start(bf16[1,128,1024]{2,1,0:T(8,128)(2,1)} %get-tuple-element.128), channel_id=1, source_target_pairs={{0,6},{1,7},{2,4},{3,5},{4,2},{5,3},{6,0},{7,1},{8,14},{9,15},{10,... | collective-permute-start | bytes 786440 | tf_op jit(solution)/shard_map/ppermute | solution.py:111
  37.1 27.2 %collective-permute-start.6 = (bf16[1,128,1024]{2,1,0:T(8,128)(2,1)S(1)}, bf16[1,128,1024]{2,1,0:T(8,128)(2,1)S(1)}, u32[]{:S(2)}, u32[]{:S(2)}) collective-permute-start(bf16[1,128,1024]{2,1,0:T(8,128)(2,1)S(1)} %get-tuple-element.127), channel_id=1, source_target_pairs={{0,7},{1,6},{2,5},{3,4},{4,3},{5,2},{6,1},{7,0},{8,15},{9,14},{10,... | collective-permute-start | bytes 786440 | tf_op jit(solution)/shard_map/ppermute | solution.py:111
  41.9 23.6 %collective-permute-start.7 = (bf16[1,128,1024]{2,1,0:T(8,128)(2,1)S(1)}, bf16[1,128,1024]{2,1,0:T(8,128)(2,1)S(1)}, u32[]{:S(2)}, u32[]{:S(2)}) collective-permute-start(bf16[1,128,1024]{2,1,0:T(8,128)(2,1)S(1)} %get-tuple-element.126), channel_id=1, source_target_pairs={{0,8},{1,9},{2,10},{3,11},{4,12},{5,13},{6,14},{7,15},{8,0},{9,1},... | collective-permute-start | bytes 786440 | tf_op jit(solution)/shard_map/ppermute | solution.py:111
  46.2 44.3 %collective-permute-start.8 = (bf16[1,128,1024]{2,1,0:T(8,128)(2,1)S(1)}, bf16[1,128,1024]{2,1,0:T(8,128)(2,1)S(1)}, u32[]{:S(2)}, u32[]{:S(2)}) collective-permute-start(bf16[1,128,1024]{2,1,0:T(8,128)(2,1)S(1)} %get-tuple-element.125), channel_id=1, source_target_pairs={{0,9},{1,8},{2,11},{3,10},{4,13},{5,12},{6,15},{7,14},{8,1},{9,0},... | collective-permute-start | bytes 786440 | tf_op jit(solution)/shard_map/ppermute | solution.py:111
  48.0 53.7 %collective-permute-start.9 = (bf16[1,128,1024]{2,1,0:T(8,128)(2,1)S(1)}, bf16[1,128,1024]{2,1,0:T(8,128)(2,1)S(1)}, u32[]{:S(2)}, u32[]{:S(2)}) collective-permute-start(bf16[1,128,1024]{2,1,0:T(8,128)(2,1)S(1)} %get-tuple-element.124), channel_id=1, source_target_pairs={{0,10},{1,11},{2,8},{3,9},{4,14},{5,15},{6,12},{7,13},{8,2},{9,3},... | collective-permute-start | bytes 786440 | tf_op jit(solution)/shard_map/ppermute | solution.py:111
  59.4 47.8 %collective-permute-start.10 = (bf16[1,128,1024]{2,1,0:T(8,128)(2,1)S(1)}, bf16[1,128,1024]{2,1,0:T(8,128)(2,1)S(1)}, u32[]{:S(2)}, u32[]{:S(2)}) collective-permute-start(bf16[1,128,1024]{2,1,0:T(8,128)(2,1)S(1)} %get-tuple-element.123), channel_id=1, source_target_pairs={{0,11},{1,10},{2,9},{3,8},{4,15},{5,14},{6,13},{7,12},{8,3},{9,2},... | collective-permute-start | bytes 786440 | tf_op jit(solution)/shard_map/ppermute | solution.py:111
  64.3 54.3 %collective-permute-start.11 = (bf16[1,128,1024]{2,1,0:T(8,128)(2,1)S(1)}, bf16[1,128,1024]{2,1,0:T(8,128)(2,1)S(1)}, u32[]{:S(2)}, u32[]{:S(2)}) collective-permute-start(bf16[1,128,1024]{2,1,0:T(8,128)(2,1)S(1)} %get-tuple-element.122), channel_id=1, source_target_pairs={{0,12},{1,13},{2,14},{3,15},{4,8},{5,9},{6,10},{7,11},{8,4},{9,5},... | collective-permute-start | bytes 786440 | tf_op jit(solution)/shard_map/ppermute | solution.py:111
  65.5 58.7 %collective-permute-start.12 = (bf16[1,128,1024]{2,1,0:T(8,128)(2,1)S(1)}, bf16[1,128,1024]{2,1,0:T(8,128)(2,1)S(1)}, u32[]{:S(2)}, u32[]{:S(2)}) collective-permute-start(bf16[1,128,1024]{2,1,0:T(8,128)(2,1)S(1)} %get-tuple-element.121), channel_id=1, source_target_pairs={{0,13},{1,12},{2,15},{3,14},{4,9},{5,8},{6,11},{7,10},{8,5},{9,4},... | collective-permute-start | bytes 786440 | tf_op jit(solution)/shard_map/ppermute | solution.py:111
  90.5 39.3 %collective-permute-start.13 = (bf16[1,128,1024]{2,1,0:T(8,128)(2,1)S(1)}, bf16[1,128,1024]{2,1,0:T(8,128)(2,1)S(1)}, u32[]{:S(2)}, u32[]{:S(2)}) collective-permute-start(bf16[1,128,1024]{2,1,0:T(8,128)(2,1)S(1)} %get-tuple-element.120), channel_id=1, source_target_pairs={{0,14},{1,15},{2,12},{3,13},{4,10},{5,11},{6,8},{7,9},{8,6},{9,7},... | collective-permute-start | bytes 786440 | tf_op jit(solution)/shard_map/ppermute | solution.py:111
  101.7 33.3 %collective-permute-start.14 = (bf16[1,128,1024]{2,1,0:T(8,128)(2,1)S(1)}, bf16[1,128,1024]{2,1,0:T(8,128)(2,1)S(1)}, u32[]{:S(2)}, u32[]{:S(2)}) collective-permute-start(bf16[1,128,1024]{2,1,0:T(8,128)(2,1)S(1)} %get-tuple-element.119), channel_id=1, source_target_pairs={{0,15},{1,14},{2,13},{3,12},{4,11},{5,10},{6,9},{7,8},{8,7},{9,6},... | collective-permute-start | bytes 786440 | tf_op jit(solution)/shard_map/ppermute | solution.py:111
  158.5 9.8 %copy-start.8 = (s32[16,3]{0,1:T(4,128)S(1)}, s32[16,3]{0,1:T(4,128)}, u32[]{:S(2)}) copy-start(s32[16,3]{0,1:T(4,128)} %param.22) | copy-start | bytes 580
  158.5 10.0 %copy-start.10 = (f32[8]{0:T(128)S(1)}, f32[8]{0:T(128)}, u32[]{:S(2)}) copy-start(f32[8]{0:T(128)} %param.21) | copy-start | bytes 100
  158.5 95.2 %collective-permute-start.15 = (bf16[2,16,128,512]{2,3,1,0:T(8,128)(2,1)}, bf16[2,16,128,512]{2,3,1,0:T(8,128)(2,1)}, u32[]{:S(2)}, u32[]{:S(2)}) collective-permute-start(bf16[2,16,128,512]{2,3,1,0:T(8,128)(2,1)} %pad_maximum_fusion.2), channel_id=1, source_target_pairs={{0,1},{1,2},{2,3},{3,4},{4,5},{5,6},{6,7},{7,8},{8,9},{9,10},{10,1... | collective-permute-start | bytes 12582920 | tf_op jit(solution)/shard_map/ppermute | solution.py:18
  160.5 93.2 %collective-permute-start.16 = (bf16[2,16,128,512]{2,3,1,0:T(8,128)(2,1)}, bf16[2,16,128,512]{2,3,1,0:T(8,128)(2,1)}, u32[]{:S(2)}, u32[]{:S(2)}) collective-permute-start(bf16[2,16,128,512]{2,3,1,0:T(8,128)(2,1)} %pad_maximum_fusion.2), channel_id=1, source_target_pairs={{1,0},{2,1},{3,2},{4,3},{5,4},{6,5},{7,6},{8,7},{9,8},{10,9},{11,1... | collective-permute-start | bytes 12582920 | tf_op jit(solution)/shard_map/ppermute | solution.py:19
  268.5 5.9 %copy-start.2 = (f32[4,8,128,384]{3,2,1,0:T(8,128)}, f32[4,8,128,384]{3,2,1,0:T(8,128)S(1)}, u32[]{:S(2)}) copy-start(f32[4,8,128,384]{3,2,1,0:T(8,128)S(1)} %get-tuple-element.192) | copy-start | bytes 18874372 | tf_op jit(solution)/shard_map/while
  286.7 6.0 %copy-start.2 = (f32[4,8,128,384]{3,2,1,0:T(8,128)}, f32[4,8,128,384]{3,2,1,0:T(8,128)S(1)}, u32[]{:S(2)}) copy-start(f32[4,8,128,384]{3,2,1,0:T(8,128)S(1)} %get-tuple-element.192) | copy-start | bytes 18874372 | tf_op jit(solution)/shard_map/while
  305.0 6.0 %copy-start.2 = (f32[4,8,128,384]{3,2,1,0:T(8,128)}, f32[4,8,128,384]{3,2,1,0:T(8,128)S(1)}, u32[]{:S(2)}) copy-start(f32[4,8,128,384]{3,2,1,0:T(8,128)S(1)} %get-tuple-element.192) | copy-start | bytes 18874372 | tf_op jit(solution)/shard_map/while
  323.3 6.0 %copy-start.2 = (f32[4,8,128,384]{3,2,1,0:T(8,128)}, f32[4,8,128,384]{3,2,1,0:T(8,128)S(1)}, u32[]{:S(2)}) copy-start(f32[4,8,128,384]{3,2,1,0:T(8,128)S(1)} %get-tuple-element.192) | copy-start | bytes 18874372 | tf_op jit(solution)/shard_map/while
  338.9 99.1 %slice-start = ((s8[6291456]{0:T(1024)(128)(4,1)}), s8[4194304]{0:T(1024)(128)(4,1)S(1)}, s32[]{:S(2)}) async-start(s8[6291456]{0:T(1024)(128)(4,1)} %bitcast.119), calls=%async_computation | async-start | bytes 8388608
  338.9 99.1 %slice-start.2 = ((s8[6291456]{0:T(1024)(128)(4,1)}), s8[4194304]{0:T(1024)(128)(4,1)S(1)}, s32[]{:S(2)}) async-start(s8[6291456]{0:T(1024)(128)(4,1)} %bitcast.123), calls=%async_computation.2 | async-start | bytes 8388608
  338.9 99.1 %slice-start.1 = ((s8[6291456]{0:T(1024)(128)(4,1)}), s8[2097152]{0:T(1024)(128)(4,1)S(1)}, s32[]{:S(2)}) async-start(s8[6291456]{0:T(1024)(128)(4,1)} %bitcast.119), calls=%async_computation.1 | async-start | bytes 4194304
  338.9 99.1 %slice-start.3 = ((s8[6291456]{0:T(1024)(128)(4,1)}), s8[2097152]{0:T(1024)(128)(4,1)S(1)}, s32[]{:S(2)}) async-start(s8[6291456]{0:T(1024)(128)(4,1)} %bitcast.123), calls=%async_computation.3 | async-start | bytes 4194304
  342.9 95.0 %collective-permute-start.17 = (bf16[2,16,128,512]{2,3,1,0:T(8,128)(2,1)S(1)}, bf16[2,16,128,512]{2,3,1,0:T(8,128)(2,1)S(1)}, u32[]{:S(2)}, u32[]{:S(2)}) collective-permute-start(bf16[2,16,128,512]{2,3,1,0:T(8,128)(2,1)S(1)} %get-tuple-element.113), channel_id=1, source_target_pairs={{0,1},{1,2},{2,3},{3,4},{4,5},{5,6},{6,7},{7,8},{8,9},{9,10},{10,1... | collective-permute-start | bytes 12582920 | tf_op jit(solution)/shard_map/ppermute | solution.py:27
  345.3 92.7 %collective-permute-start.18 = (bf16[2,16,128,512]{2,3,1,0:T(8,128)(2,1)S(1)}, bf16[2,16,128,512]{2,3,1,0:T(8,128)(2,1)S(1)}, u32[]{:S(2)}, u32[]{:S(2)}) collective-permute-start(bf16[2,16,128,512]{2,3,1,0:T(8,128)(2,1)S(1)} %get-tuple-element.114), channel_id=1, source_target_pairs={{1,0},{2,1},{3,2},{4,3},{5,4},{6,5},{7,6},{8,7},{9,8},{10,9},{11,1... | collective-permute-start | bytes 12582920 | tf_op jit(solution)/shard_map/ppermute | solution.py:27
  441.6 6.6 %copy-start.1 = (bf16[1024,512]{1,0:T(8,128)(2,1)S(1)}, bf16[1024,512]{1,0:T(8,128)(2,1)}, u32[]{:S(2)}) copy-start(bf16[1024,512]{1,0:T(8,128)(2,1)} %param.19) | copy-start | bytes 3145732
  (8 other events, 27.1 us)
